TPU v7x, 512 devices: a whole 4x8x8 slice. The times are simulated.
512 devices in a mesh: grp: 16 (over y, core), ops: 32 (over x, z).
Axes of the slice: x: 4, y: 8, z: 8, core: 2. Of those that a mesh axis runs over, the one named last changes fastest.
Arguments:
- op_embed: bfloat16 [131072, 256], P(('grp', 'ops')), may hold values from -6 to 6
- machine_embed: bfloat16 [8192, 256], P('grp'), may hold values from -6 to 6
- cotangent: bfloat16 [131072, 256], P(('grp', 'ops')), may hold values from -6 to 6
- w_query: bfloat16 [256, 256], replicated, may hold values from -0.375 to 0.375
- w_key: bfloat16 [256, 256], replicated, may hold values from -0.375 to 0.375
- w_value: bfloat16 [256, 256], replicated, may hold values from -0.375 to 0.375
- slot_local: int32 [512, 16], P(('grp', 'ops')), may hold values from 0 to 3
- counts: int32 [131072, 16], P(('grp', 'ops')), may hold values from 0 to 128, as said below
Outputs:
- op_grad: bfloat16 [131072, 256], P(('grp', 'ops'))
- machine_grad: float32 [8192, 256], P(('grp', 'ops'))
- grad_wq: float32 [256, 256], replicated
- grad_wk: float32 [256, 256], replicated
- grad_wv: float32 [256, 256], replicated
Inputs may be any that keep to these rules, and one draw needn't show every extreme that they name: The eligible machines of slot e's block for operation o are its first counts[o, e] machines; 0 means the operation has no eligible machine in that block.
All inputs are finite; a program needn't handle non-finite values.
Results may differ from a plain program's by a relative error of at most 0.0056.
Values may be sent and summed in bfloat16 or wider, within the bound.
No kernel may reach another device: no remote copies, remote signals or barrier semaphores. Data moves between devices by JAX's collectives and lax.ppermute only.
A program may use at most 64 MiB of HBM per device.

v0:
```python
import jax
import jax.numpy as jnp
from jax import lax
from jax.sharding import PartitionSpec as P

HEADS = 8
BLK = 128
mean_scale = 0.08838834764831845


def slot_grads(queries, cotangent4, key_rows, value_rows, lengths):
    head_size = queries.shape[2]
    inv_root = head_size ** (-0.5)
    scores = (
        jnp.einsum("ohc,mhc->ohm", queries, key_rows, preferred_element_type=jnp.float32) * inv_root
    )
    sigmoid_score = jax.nn.sigmoid(scores)
    columns = lax.broadcasted_iota(jnp.int32, scores.shape, 2)
    eligible = columns < lengths[:, None, None]
    gates = jnp.where(eligible, sigmoid_score, 0.0).astype(jnp.bfloat16)
    value_dot = jnp.einsum(
        "ohc,mhc->ohm", cotangent4, value_rows, preferred_element_type=jnp.float32
    )
    dscore = jnp.where(
        eligible, mean_scale * value_dot * sigmoid_score * (1.0 - sigmoid_score) * inv_root, 0.0
    ).astype(jnp.bfloat16)
    query_part = jnp.einsum("ohm,mhc->ohc", dscore, key_rows, preferred_element_type=jnp.float32)
    key_grad = jnp.einsum(
        "ohm,ohc->mhc", dscore, queries, preferred_element_type=jnp.float32
    ).astype(jnp.bfloat16)
    value_grad = (
        mean_scale
        * jnp.einsum("ohm,ohc->mhc", gates, cotangent4, preferred_element_type=jnp.float32)
    ).astype(jnp.bfloat16)
    return (query_part, key_grad, value_grad)


def per_device(op_embed, machine_embed, cotangent, w_query, w_key, w_value, slot_local, counts):
    groups = lax.axis_size("grp")
    ops_count = op_embed.shape[0]
    model_width = op_embed.shape[1]
    head_size = model_width // HEADS
    machine_rows = machine_embed.shape[0]
    blocks_here = machine_rows // BLK
    highest = lax.Precision.HIGHEST
    both_weights = jnp.concatenate([w_key, w_value], axis=1)
    queries = jnp.dot(op_embed, w_query, preferred_element_type=jnp.float32).astype(jnp.bfloat16)
    wanted = lax.all_to_all(
        slot_local.reshape(groups, 1), "grp", split_axis=0, concat_axis=0, tiled=True
    )
    wanted_ids = wanted[:, 0]
    picker = wanted_ids[:, None] == jnp.arange(blocks_here, dtype=jnp.int32)[None, :]
    local_pairs = jnp.dot(machine_embed, both_weights, preferred_element_type=jnp.float32).astype(
        jnp.bfloat16
    )
    outgoing = local_pairs.reshape(blocks_here, BLK, 2 * model_width)[wanted_ids]
    fetched = lax.all_to_all(outgoing, "grp", split_axis=0, concat_axis=0, tiled=True)
    key_slots = fetched[:, :, :model_width].reshape(groups, BLK, HEADS, head_size)
    value_slots = fetched[:, :, model_width:].reshape(groups, BLK, HEADS, head_size)
    query_heads = queries.reshape(ops_count, HEADS, head_size)
    cot_heads = cotangent.reshape(ops_count, HEADS, head_size)

    def per_slot(summed_q, pieces):
        key_rows, value_rows, lengths = pieces
        query_part, key_grad, value_grad = slot_grads(
            query_heads, cot_heads, key_rows, value_rows, lengths
        )
        return (
            summed_q + query_part,
            (key_grad.reshape(BLK, model_width), value_grad.reshape(BLK, model_width)),
        )

    start_q = jnp.zeros((ops_count, HEADS, head_size), jnp.float32)
    summed_q, (key_grads, value_grads) = lax.scan(
        per_slot, start_q, (key_slots, value_slots, counts.T)
    )
    grad_query = summed_q.astype(jnp.bfloat16).reshape(ops_count, model_width)
    op_grad = (
        cotangent.astype(jnp.float32)
        + jnp.dot(grad_query, w_query.T, preferred_element_type=jnp.float32)
    ).astype(jnp.bfloat16)
    wq_term = jnp.einsum("od,oe->de", op_embed, grad_query, preferred_element_type=jnp.float32)
    returned = lax.all_to_all(
        jnp.concatenate([key_grads, value_grads], axis=2),
        "grp",
        split_axis=0,
        concat_axis=0,
        tiled=True,
    )
    summed = jnp.einsum(
        "gb,gr->br",
        picker.astype(jnp.bfloat16),
        returned.reshape(groups, BLK * 2 * model_width),
        preferred_element_type=jnp.float32,
    )
    summed = summed.reshape(machine_rows, 2 * model_width)
    key_total = summed[:, :model_width]
    value_total = summed[:, model_width:]
    machine_part = jnp.dot(key_total, w_key.astype(jnp.float32).T, precision=highest) + jnp.dot(
        value_total, w_value.astype(jnp.float32).T, precision=highest
    )
    embed_f = machine_embed.astype(jnp.float32)
    wk_term = jnp.dot(embed_f.T, key_total, precision=highest)
    wv_term = jnp.dot(embed_f.T, value_total, precision=highest)
    summed_total = lax.psum(machine_part, "ops")
    share_rows = machine_rows // lax.axis_size("ops")
    first_row = lax.axis_index("ops") * share_rows
    machine_grad = lax.dynamic_slice_in_dim(summed_total, first_row, share_rows, 0)
    weight_sums = lax.psum((wq_term, wk_term, wv_term), ("grp", "ops"))
    shard_count = float(groups * lax.axis_size("ops"))
    grad_wq = weight_sums[0] / shard_count
    grad_wk = weight_sums[1] / shard_count
    grad_wv = weight_sums[2] / shard_count
    return (op_grad, machine_grad, grad_wq, grad_wk, grad_wv)


def solution(mesh):
    return jax.shard_map(
        per_device,
        mesh=mesh,
        in_specs=(
            P(("grp", "ops"), None),
            P("grp", None),
            P(("grp", "ops"), None),
            P(),
            P(),
            P(),
            P(("grp", "ops"), None),
            P(("grp", "ops"), None),
        ),
        out_specs=(P(("grp", "ops"), None), P(("grp", "ops"), None), P(), P(), P()),
        check_vma=False,
    )
```

profile of v0, /device:TPU:8, one launch (start us, length us, event | category | flops | bytes accessed | tf_op | source)
XLA Modules:
  0.0 657.2 jit_solution(9235457132968034616)
XLA Ops:
  7.2 1.4 copy.46
  8.6 9.1 %all-to-all-start = ((s32[16,1,1]{2,1,0:T(1,128)}), s32[16,1,1]{2,1,0:T(1,128)S(1)}, u32[]{:S(2)}, u32[]{:S(2)}) async-start(s32[16,1,1]{2,1,0:T(1,128)} %copy.46), calls=%async_computation | async-start | bytes 16384 | tf_op jit(solution)/shard_map/all_to_all | solution.py:48
  18.9 4.9 all-to-all-done
  24.2 2.0 gather_fusion
  26.2 5.1 all-to-all-start.1
  31.7 46.8 %all-to-all-done.1 = bf16[16,128,512]{2,1,0:T(8,128)(2,1)S(1)} async-done(((bf16[16,128,512]{2,1,0:T(8,128)(2,1)}), bf16[16,128,512]{2,1,0:T(8,128)(2,1)S(1)}, u32[]{:S(2)}, u32[]{:S(2)}) %all-to-all-start.1) | async-done | bytes 2097184 | tf_op jit(solution)/shard_map/all_to_all | solution.py:57
  78.6 1.6 fusion.38
  80.2 1.7 copy.47
  81.9 1.3 copy.48
  83.2 63.6 %while.15 = (s32[]{:T(128)}, f32[256,8,32]{0,2,1:T(8,128)S(1)}, bf16[16,128,256]{1,2,0:T(8,128)(2,1)}, bf16[16,128,256]{1,2,0:T(8,128)(2,1)}, bf16[16,128,8,32]{...) while((s32[]{:T(128)}, f32[256,8,32]{0,2,1:T(8,128)S(1)}, ...), condition=%wide.region_1.2_spmd.clone, body=%wide.region_0.1_spmd.clone.sunk | while | flops 87785472 | bytes 6361235 | solution.py:74
  88.4 1.3 fusion.80
  92.4 1.3 fusion.80
  100.3 1.3 fusion.80
  128.1 1.3 fusion.80
  132.1 1.3 fusion.80
  140.1 1.3 fusion.80
  144.0 1.3 fusion.80
  146.8 3.1 pad_maximum_fusion
  149.9 6.9 %all-to-all-start.2 = ((bf16[16,128,512]{1,2,0:T(8,128)(2,1)}), bf16[16,128,512]{1,2,0:T(8,128)(2,1)}, u32[]{:S(2)}, u32[]{:S(2)}) async-start(bf16[16,128,512]{1,2,0:T(8,128)(2,1)} %pad_maximum_fusion), calls=%async_computation.2 | async-start | bytes 4194304 | tf_op jit(solution)/shard_map/all_to_all | solution.py:83
  157.7 46.3 %all-to-all-done.2 = bf16[16,128,512]{1,2,0:T(8,128)(2,1)} async-done(((bf16[16,128,512]{1,2,0:T(8,128)(2,1)}), bf16[16,128,512]{1,2,0:T(8,128)(2,1)}, u32[]{:S(2)}, u32[]{:S(2)}) %all-to-all-start.2) | async-done | bytes 2097184 | tf_op jit(solution)/shard_map/all_to_all | solution.py:83
  204.0 3.4 copy.57
  214.0 274.6 %all-reduce.6.cloned.1.call-done = (f32[256,256]{0,1:T(8,128)}, f32[256,256]{0,1:T(8,128)}, f32[256,256]{0,1:T(8,128)}) async-done(((f32[256,256]{0,1:T(8,128)}, f32[256,256]{0,1:T(8,128)}, f32[256,256]{0,1:T(8,128)}), (f32[256,256]{0,1:T(8,128)}, f32[256,256]{0,1:T(8,128)}, f32[256,256]{0,1:T(8,128)})) %all-reduce.6.cloned.1.call-update) | async-done | bytes 786448 | tf_op jit(solution)/shard_map/psum | solution.py:109
  493.2 155.8 %all-reduce.4.cloned.1.call-done = f32[512,256]{1,0:T(8,128)} async-done(((f32[512,256]{1,0:T(8,128)}), f32[512,256]{1,0:T(8,128)}) %all-reduce.4.cloned.1.call-update) | async-done | bytes 524304 | tf_op jit(solution)/shard_map/psum | solution.py:105
  649.0 1.3 constant_dynamic-slice_fusion.1
  (152 shorter events, 68.0 us)
Async XLA Ops:
  7.2 10.5 %copy-start = (bf16[512,256]{1,0:T(8,128)(2,1)S(1)}, bf16[512,256]{1,0:T(8,128)(2,1)}, u32[]{:S(2)}) copy-start(bf16[512,256]{1,0:T(8,128)(2,1)} %param.11) | copy-start | bytes 786436
  8.6 15.3 %all-to-all-start = ((s32[16,1,1]{2,1,0:T(1,128)}), s32[16,1,1]{2,1,0:T(1,128)S(1)}, u32[]{:S(2)}, u32[]{:S(2)}) async-start(s32[16,1,1]{2,1,0:T(1,128)} %copy.46), calls=%async_computation | async-start | bytes 16384 | tf_op jit(solution)/shard_map/all_to_all | solution.py:48
  26.2 5.1 copy-start.6
  26.2 5.3 copy-start.2
  26.2 5.3 copy-start.4
  26.2 52.3 %all-to-all-start.1 = ((bf16[16,128,512]{2,1,0:T(8,128)(2,1)}), bf16[16,128,512]{2,1,0:T(8,128)(2,1)S(1)}, u32[]{:S(2)}, u32[]{:S(2)}) async-start(bf16[16,128,512]{2,1,0:T(8,128)(2,1)} %gather_fusion), calls=%async_computation.1 | async-start | bytes 4194304 | tf_op jit(solution)/shard_map/all_to_all | solution.py:57
  80.2 1.7 copy-start.1
  149.9 6.9 %copy-start.3 = (bf16[256,256]{1,0:T(8,128)(2,1)S(1)}, bf16[256,256]{1,0:T(8,128)(2,1)}, u32[]{:S(2)}) copy-start(bf16[256,256]{1,0:T(8,128)(2,1)} %param.10) | copy-start | bytes 393220
  149.9 54.2 %all-to-all-start.2 = ((bf16[16,128,512]{1,2,0:T(8,128)(2,1)}), bf16[16,128,512]{1,2,0:T(8,128)(2,1)}, u32[]{:S(2)}, u32[]{:S(2)}) async-start(bf16[16,128,512]{1,2,0:T(8,128)(2,1)} %pad_maximum_fusion), calls=%async_computation.2 | async-start | bytes 4194304 | tf_op jit(solution)/shard_map/all_to_all | solution.py:83
  156.8 331.9 %all-reduce.6.cloned.1.call-start = ((), (), s32[]{:S(2)}) async-start(), calls=%async_computation.4 | async-start | bytes 1572864 | tf_op jit(solution)/shard_map/psum | solution.py:109
  208.0 3.4 copy-start.8
  208.7 3.1 copy-start.9
  211.3 1.8 copy-start.5
  211.3 1.8 copy-start.7
  211.4 437.6 %all-reduce.4.cloned.1.call-start = ((), (), s32[]{:S(2)}) async-start(), calls=%async_computation.3 | async-start | bytes 1048576 | tf_op jit(solution)/shard_map/psum | solution.py:105
Sparse Core Ops, SparseCore 0:
  211.5 277.0 all-reduce.5
  492.0 156.9 all-reduce.3
where the time goes:
time: 659 us; the launch traced here: 657 us
  waiting for transfers between devices  529 us (80%)
  matrix products  48.8 us (7%)
  local copies, waits for them, and re-layouts  38.4 us (6%)
  starting transfers between devices  21.1 us (3%)
  between operations  14.3 us (2%)
    psum x1, waiting for transfers between devices, per_device(): weight_sums = lax.psum((wq_term, wk_term, wv_term), ('grp', 'ops'))  275 us
    psum x1, waiting for transfers between devices, per_device(): summed_total = lax.psum(machine_part, 'ops')  156 us
    all_to_all x1, waiting for transfers between devices, per_device(): lax.all_to_all(outgoing, 'grp', split_axis=0, concat_axis=0, tiled=True)  46.8 us
    all_to_all x1, waiting for transfers between devices, per_device(): lax.all_to_all(jnp.concatenate([key_grads, value_grads], axis=2), 'grp',...  46.3 us
    dot_general x16, matrix products, slot_grads(): jnp.einsum('ohc,mhc->ohm', cotangent4, value_rows, preferred_element_type...  20.9 us
  transfers between devices with their start and end apart: 5, of which 5 were waited for; matrix products, arithmetic and copies ran while one was open for 1% of the time, Pallas kernels for 0%

commit v1 on v0

--- a/solution.py
+++ b/solution.py
@@ -106,7 +106,7 @@
     share_rows = machine_rows // lax.axis_size("ops")
     first_row = lax.axis_index("ops") * share_rows
     machine_grad = lax.dynamic_slice_in_dim(summed_total, first_row, share_rows, 0)
-    weight_sums = lax.psum((wq_term, wk_term, wv_term), ("grp", "ops"))
+    weight_sums = lax.psum(lax.psum((wq_term, wk_term, wv_term), "grp"), "ops")
     shard_count = float(groups * lax.axis_size("ops"))
     grad_wq = weight_sums[0] / shard_count
     grad_wk = weight_sums[1] / shard_count

time: 659 us -> 527 us (0.80)
  waiting for transfers between devices: 529 us -> 383 us
  matrix products: 48.8 us -> 62.4 us
    psum x1, waiting for transfers between devices: 275 us -> 116 us  [per_device(): weight_sums = lax.psum(lax.psum((wq_term, wk_term, wv_term), 'grp'), 'ops')]
    dot_general x16, matrix products: 3.44 us -> 16.9 us  [slot_grads(): jnp.einsum('ohm,mhc->ohc', dscore, key_rows, preferred_element_type=jnp.f...]
    dot_general x16, matrix products: 7.87 us -> 21.3 us  [slot_grads(): jnp.einsum('ohc,mhc->ohm', queries, key_rows, preferred_element_type=jnp....]
    dot_general x16, matrix products: 20.9 us -> 7.52 us  [slot_grads(): jnp.einsum('ohc,mhc->ohm', cotangent4, value_rows, preferred_element_type...]
    psum x1, waiting for transfers between devices: 156 us -> 169 us  [per_device(): summed_total = lax.psum(machine_part, 'ops')]
where the time goes in v1:
time: 527 us; the launch traced here: 525 us
  waiting for transfers between devices  383 us (73%)
  matrix products  62.4 us (12%)
  local copies, waits for them, and re-layouts  37.4 us (7%)
  starting transfers between devices  21.7 us (4%)
  between operations  14.3 us (3%)
  other arithmetic  5.53 us (1%)
    psum x1, waiting for transfers between devices, per_device(): summed_total = lax.psum(machine_part, 'ops')  169 us
    psum x1, waiting for transfers between devices, per_device(): weight_sums = lax.psum(lax.psum((wq_term, wk_term, wv_term), 'grp'), 'ops')  116 us
    all_to_all x1, waiting for transfers between devices, per_device(): lax.all_to_all(outgoing, 'grp', split_axis=0, concat_axis=0, tiled=True)  46.9 us
    all_to_all x1, waiting for transfers between devices, per_device(): lax.all_to_all(jnp.concatenate([key_grads, value_grads], axis=2), 'grp',...  46.3 us
    dot_general x16, matrix products, slot_grads(): jnp.einsum('ohc,mhc->ohm', queries, key_rows, preferred_element_type=jnp....  21.3 us
    dot_general x16, matrix products, slot_grads(): jnp.einsum('ohm,mhc->ohc', dscore, key_rows, preferred_element_type=jnp.f...  16.9 us
    dynamic_slice x16, local copies, waits for them, and re-layouts, per_device(): lax.scan(per_slot, start_q, (key_slots, value_slots, counts.T))  11.3 us
    dynamic_update_slice x16, local copies, waits for them, and re-layouts, per_device(): lax.scan(per_slot, start_q, (key_slots, value_slots, counts.T))  11 us
  transfers between devices with their start and end apart: 5, of which 5 were waited for; matrix products, arithmetic and copies ran while one was open for 1% of the time, Pallas kernels for 0%

profile of v1, /device:TPU:8, one launch (start us, length us, event | category | flops | bytes accessed | tf_op | source)
XLA Modules:
  0.0 524.8 jit_solution(10441471081754524153)
XLA Ops:
  7.2 1.4 copy.46
  8.6 9.1 %all-to-all-start = ((s32[16,1,1]{2,1,0:T(1,128)}), s32[16,1,1]{2,1,0:T(1,128)S(1)}, u32[]{:S(2)}, u32[]{:S(2)}) async-start(s32[16,1,1]{2,1,0:T(1,128)} %copy.46), calls=%async_computation | async-start | bytes 16384 | tf_op jit(solution)/shard_map/all_to_all | solution.py:48
  18.9 4.9 all-to-all-done
  24.2 2.0 gather_fusion
  26.2 5.8 %all-to-all-start.1 = ((bf16[16,128,512]{2,1,0:T(8,128)(2,1)}), bf16[16,128,512]{2,1,0:T(8,128)(2,1)}, u32[]{:S(2)}, u32[]{:S(2)}) async-start(bf16[16,128,512]{2,1,0:T(8,128)(2,1)} %gather_fusion), calls=%async_computation.1 | async-start | bytes 4194304 | tf_op jit(solution)/shard_map/all_to_all | solution.py:57
  32.4 46.9 %all-to-all-done.1 = bf16[16,128,512]{2,1,0:T(8,128)(2,1)} async-done(((bf16[16,128,512]{2,1,0:T(8,128)(2,1)}), bf16[16,128,512]{2,1,0:T(8,128)(2,1)}, u32[]{:S(2)}, u32[]{:S(2)}) %all-to-all-start.1) | async-done | bytes 2097184 | tf_op jit(solution)/shard_map/all_to_all | solution.py:57
  79.3 1.7 fusion.38
  83.0 77.1 %while.15 = (s32[]{:T(128)}, f32[256,8,32]{0,2,1:T(8,128)S(1)}, bf16[16,128,256]{1,2,0:T(8,128)(2,1)}, bf16[16,128,256]{1,2,0:T(8,128)(2,1)}, bf16[16,128,8,32]{...) while((s32[]{:T(128)}, f32[256,8,32]{0,2,1:T(8,128)S(1)}, ...), condition=%wide.region_1.2_spmd.clone, body=%wide.region_0.1_spmd.clone.sunk | while | flops 87785472 | bytes 6361235 | solution.py:74
  83.0 1.3 fusion.79
  87.8 1.3 fusion.79
  92.6 1.3 fusion.79
  97.4 1.3 fusion.79
  102.3 1.3 fusion.79
  107.1 1.3 fusion.79
  111.9 1.3 fusion.79
  131.2 1.3 fusion.79
  136.0 1.3 fusion.79
  140.8 1.3 fusion.79
  160.1 3.1 pad_maximum_fusion
  163.2 6.7 %all-to-all-start.2 = ((bf16[16,128,512]{1,2,0:T(8,128)(2,1)}), bf16[16,128,512]{1,2,0:T(8,128)(2,1)}, u32[]{:S(2)}, u32[]{:S(2)}) async-start(bf16[16,128,512]{1,2,0:T(8,128)(2,1)} %pad_maximum_fusion), calls=%async_computation.2 | async-start | bytes 4194304 | tf_op jit(solution)/shard_map/all_to_all | solution.py:83
  170.9 46.3 %all-to-all-done.2 = bf16[16,128,512]{1,2,0:T(8,128)(2,1)} async-done(((bf16[16,128,512]{1,2,0:T(8,128)(2,1)}), bf16[16,128,512]{1,2,0:T(8,128)(2,1)}, u32[]{:S(2)}, u32[]{:S(2)}) %all-to-all-start.2) | async-done | bytes 2097184 | tf_op jit(solution)/shard_map/all_to_all | solution.py:83
  217.2 3.4 copy.57
  226.3 116.0 %all-reduce.7.cloned.1.call-done = (f32[256,256]{0,1:T(8,128)}, f32[256,256]{0,1:T(8,128)}, f32[256,256]{0,1:T(8,128)}) async-done(((f32[256,256]{0,1:T(8,128)}, f32[256,256]{0,1:T(8,128)}, f32[256,256]{0,1:T(8,128)}), (f32[256,256]{0,1:T(8,128)}, f32[256,256]{0,1:T(8,128)}, f32[256,256]{0,1:T(8,128)})) %all-reduce.7.cloned.1.call-update) | async-done | bytes 786448 | tf_op jit(solution)/shard_map/psum | solution.py:109
  343.2 168.9 %all-reduce.5.cloned.1.call-done = (f32[512,256]{1,0:T(8,128)}, f32[256,256]{0,1:T(8,128)}, f32[256,256]{0,1:T(8,128)}, f32[256,256]{0,1:T(8,128)}) async-done(((f32[512,256]{1,0:T(8,128)}, f32[256,256]{0,1:T(8,128)}, f32[256,256]{0,1:T(8,128)}, f32[256,256]{0,1:T(8,128)}), (f32[512,256]{1,0:T(8,128)}, f32[256,256]{0,1:T(8,128)}, f32[256,256]{0,1:T(8,128)}, ...) | async-done | bytes 1310736 | tf_op jit(solution)/shard_map/psum | solution.py:105
  (148 shorter events, 80.6 us)
Async XLA Ops:
  7.2 10.5 %copy-start = (bf16[512,256]{1,0:T(8,128)(2,1)S(1)}, bf16[512,256]{1,0:T(8,128)(2,1)}, u32[]{:S(2)}) copy-start(bf16[512,256]{1,0:T(8,128)(2,1)} %param.11) | copy-start | bytes 786436
  8.6 15.3 %all-to-all-start = ((s32[16,1,1]{2,1,0:T(1,128)}), s32[16,1,1]{2,1,0:T(1,128)S(1)}, u32[]{:S(2)}, u32[]{:S(2)}) async-start(s32[16,1,1]{2,1,0:T(1,128)} %copy.46), calls=%async_computation | async-start | bytes 16384 | tf_op jit(solution)/shard_map/all_to_all | solution.py:48
  26.2 5.8 %copy-start.4 = (bf16[256,256]{1,0:T(8,128)(2,1)S(1)}, bf16[256,256]{1,0:T(8,128)(2,1)}, u32[]{:S(2)}) copy-start(bf16[256,256]{1,0:T(8,128)(2,1)} %param.12) | copy-start | bytes 393220
  26.2 5.9 %copy-start.1 = (bf16[256,256]{1,0:T(8,128)(2,1)S(1)}, bf16[256,256]{1,0:T(8,128)(2,1)}, u32[]{:S(2)}) copy-start(bf16[256,256]{1,0:T(8,128)(2,1)} %param.10) | copy-start | bytes 393220
  26.2 5.9 %copy-start.2 = (bf16[256,256]{1,0:T(8,128)(2,1)S(1)}, bf16[256,256]{1,0:T(8,128)(2,1)}, u32[]{:S(2)}) copy-start(bf16[256,256]{1,0:T(8,128)(2,1)} %param.13) | copy-start | bytes 393220
  26.2 53.1 %all-to-all-start.1 = ((bf16[16,128,512]{2,1,0:T(8,128)(2,1)}), bf16[16,128,512]{2,1,0:T(8,128)(2,1)}, u32[]{:S(2)}, u32[]{:S(2)}) async-start(bf16[16,128,512]{2,1,0:T(8,128)(2,1)} %gather_fusion), calls=%async_computation.1 | async-start | bytes 4194304 | tf_op jit(solution)/shard_map/all_to_all | solution.py:57
  163.2 54.0 %all-to-all-start.2 = ((bf16[16,128,512]{1,2,0:T(8,128)(2,1)}), bf16[16,128,512]{1,2,0:T(8,128)(2,1)}, u32[]{:S(2)}, u32[]{:S(2)}) async-start(bf16[16,128,512]{1,2,0:T(8,128)(2,1)} %pad_maximum_fusion), calls=%async_computation.2 | async-start | bytes 4194304 | tf_op jit(solution)/shard_map/all_to_all | solution.py:83
  169.9 172.3 %all-reduce.7.cloned.1.call-start = ((), (), s32[]{:S(2)}) async-start(), calls=%async_computation.4 | async-start | bytes 1572864 | tf_op jit(solution)/shard_map/psum | solution.py:109
  221.2 3.4 copy-start.6
  221.9 3.1 copy-start.7
  224.5 117.8 %copy-start.3 = (bf16[256,256]{1,0:T(8,128)(2,1)S(1)}, bf16[256,256]{1,0:T(8,128)(2,1)}, u32[]{:S(2)}) copy-start(bf16[256,256]{1,0:T(8,128)(2,1)} %param.13) | copy-start | bytes 393220
  224.5 117.8 %copy-start.5 = (bf16[256,256]{1,0:T(8,128)(2,1)S(1)}, bf16[256,256]{1,0:T(8,128)(2,1)}, u32[]{:S(2)}) copy-start(bf16[256,256]{1,0:T(8,128)(2,1)} %param.12) | copy-start | bytes 393220
  224.6 287.5 %all-reduce.5.cloned.1.call-start = ((), (), s32[]{:S(2)}) async-start(), calls=%async_computation.3 | async-start | bytes 2621440 | tf_op jit(solution)/shard_map/psum | solution.py:105
Sparse Core Ops, SparseCore 0:
  224.7 117.5 all-reduce.6
  346.1 165.9 all-reduce.4
